TPU v7x, 32 devices: a whole 2x2x4 slice. The times are simulated.
32 devices in a mesh: ctx: 16 (over z, x, core), tp: 2 (over y).
Axes of the slice: x: 2, y: 2, z: 4, core: 2. Of those that a mesh axis runs over, the one named last changes fastest.
Arguments:
- token_ids: int32 [8192], P('ctx'), may hold values from 0 to 511
- embed_table: bfloat16 [512, 8192], P(None, 'tp'), may hold values from -81 to 81
- projected_table: bfloat16 [512, 3, 8192], P(None, None, 'tp'), may hold values from -10.5 to 10.5
- feat_one: float32 [3, 3, 8192], P(None, None, 'tp'), may hold values from -3 to 3
- inner_taps: float32 [7, 8192], P(None, 'tp'), may hold values from -2 to 2
- feat_two: float32 [3, 3, 8192], P(None, None, 'tp'), may hold values from -3 to 3
- decay: float32 [8192, 16], P('tp'), may hold values from 3.540039e-05 to 0.03448276
- residue: float32 [8192, 16], P('tp'), may hold values from -0.26261287 to 0.26261287
Outputs:
- stream_out: bfloat16 [8192, 8192], P('ctx', 'tp')
All inputs are finite; a program needn't handle non-finite values.
Results may differ from a plain program's by a relative error of at most 0.0048.
Values may be sent and summed in bfloat16 or wider, within the bound.
A program may use at most 320 MiB of HBM per device.

v0:
```python
import math

import jax
import jax.numpy as jnp
from jax import lax
from jax.sharding import PartitionSpec as P

D = 8192


epsilon = 1e-06
PRECISE = lax.Precision.HIGHEST


def shifted(value, axis, steps):
    count = lax.axis_size(axis)
    first, last = (max(0, -steps), min(count, count - steps))
    return lax.ppermute(value, axis, [(source, source + steps) for source in range(first, last)])


def valid_taps(series, weights):
    tap_count = weights.shape[0]
    out_rows = series.shape[0] - tap_count + 1
    summed = weights[0] * series[tap_count - 1 : tap_count - 1 + out_rows]
    for offset in range(1, tap_count):
        summed = (
            summed
            + weights[offset] * series[tap_count - 1 - offset : tap_count - 1 - offset + out_rows]
        )
    return summed


def look_up(all_ids, embed_table, projected_table):
    vocab_size = embed_table.shape[0]
    one_hot = (all_ids[:, None] == jnp.arange(vocab_size, dtype=jnp.int32)[None, :]).astype(
        jnp.bfloat16
    )
    embedded = jnp.dot(one_hot, embed_table, preferred_element_type=jnp.float32)
    flattened = projected_table.reshape(vocab_size, -1)
    raw_rows = jnp.dot(one_hot, flattened, preferred_element_type=jnp.float32)
    return (embedded, raw_rows.reshape(all_ids.shape[0], 3, -1))


def block_one(raw_rows, embedded, feat_one, inner_taps):
    queries = valid_taps(raw_rows[:, 0], feat_one[:, 0])
    key_rows = valid_taps(raw_rows[:, 1], feat_one[:, 1])
    valued = valid_taps(raw_rows[:, 2], feat_one[:, 2])
    mixture = valid_taps(key_rows * valued, inner_taps)
    out_rows = mixture.shape[0]
    return (embedded + queries[queries.shape[0] - out_rows :] * mixture).astype(jnp.bfloat16)


def split_sizes(length):
    columns = 1
    for divisor in range(1, 129):
        if length % divisor == 0:
            columns = divisor
    return (2 * length // columns, columns)


def fourier_tables(outer_len, columns):
    total_len = outer_len * columns
    rows_k = jnp.arange(outer_len, dtype=jnp.int32)
    rows_q = jnp.arange(columns, dtype=jnp.int32)
    outer_angles = (rows_k[:, None] * rows_k[None, :] % outer_len).astype(jnp.float32) * (
        2.0 * math.pi / outer_len
    )
    col_angles = (rows_q[:, None] * rows_q[None, :] % columns).astype(jnp.float32) * (
        2.0 * math.pi / columns
    )
    tw_angles = (rows_k[:, None] * rows_q[None, :] % total_len).astype(jnp.float32) * (
        2.0 * math.pi / total_len
    )
    return (
        jnp.cos(outer_angles),
        -jnp.sin(outer_angles),
        jnp.cos(col_angles),
        -jnp.sin(col_angles),
        jnp.cos(tw_angles),
        -jnp.sin(tw_angles),
    )


def first_section(table, signal):
    if signal.dtype == jnp.bfloat16:
        upper = table.astype(jnp.bfloat16)
        lower = (table - upper.astype(jnp.float32)).astype(jnp.bfloat16)
        return jnp.einsum(
            "kp,bpq->bkq", upper, signal, preferred_element_type=jnp.float32
        ) + jnp.einsum("kp,bpq->bkq", lower, signal, preferred_element_type=jnp.float32)
    return jnp.einsum("kp,bpq->bkq", table, signal, precision=PRECISE)


def forward_transform(signal, tables):
    outer_re, outer_im, col_re, col_im, tw_re, tw_im = tables
    half_rows = signal.shape[1]
    first_re = first_section(outer_re[:, :half_rows], signal)
    first_im = first_section(outer_im[:, :half_rows], signal)
    turned_re = first_re * tw_re - first_im * tw_im
    turned_im = first_re * tw_im + first_im * tw_re
    out_re = jnp.einsum("bkq,ql->bkl", turned_re, col_re, precision=PRECISE) - jnp.einsum(
        "bkq,ql->bkl", turned_im, col_im, precision=PRECISE
    )
    out_im = jnp.einsum("bkq,ql->bkl", turned_re, col_im, precision=PRECISE) + jnp.einsum(
        "bkq,ql->bkl", turned_im, col_re, precision=PRECISE
    )
    return (out_re, out_im)


def inverse_transform(spec_re, spec_im, tables):
    outer_re, outer_im, col_re, col_im, tw_re, tw_im = tables
    outer_len = outer_re.shape[0]
    total_len = outer_len * col_re.shape[0]
    half_rows = outer_len // 2
    back_re = jnp.einsum("bkl,lq->bkq", spec_re, col_re, precision=PRECISE) + jnp.einsum(
        "bkl,lq->bkq", spec_im, col_im, precision=PRECISE
    )
    back_im = jnp.einsum("bkl,lq->bkq", spec_im, col_re, precision=PRECISE) - jnp.einsum(
        "bkl,lq->bkq", spec_re, col_im, precision=PRECISE
    )
    turn_re = back_re * tw_re + back_im * tw_im
    turn_im = back_im * tw_re - back_re * tw_im
    result = jnp.einsum(
        "pk,bkq->bpq", outer_re[:half_rows], turn_re, precision=PRECISE
    ) + jnp.einsum("pk,bkq->bpq", outer_im[:half_rows], turn_im, precision=PRECISE)
    return result / total_len


def causal_convolve(series, response):
    channels, length = series.shape
    outer_len, columns = split_sizes(length)
    tables = fourier_tables(outer_len, columns)
    half_rows = outer_len // 2
    sig_re, sig_im = forward_transform(series.reshape(channels, half_rows, columns), tables)
    fil_re, fil_im = forward_transform(response.reshape(channels, half_rows, columns), tables)
    prod_re = sig_re * fil_re - sig_im * fil_im
    prod_im = sig_re * fil_im + sig_im * fil_re
    return inverse_transform(prod_re, prod_im, tables).reshape(channels, length)


def mode_response(decay, residue, length, offset):
    positions = jnp.arange(length, dtype=jnp.int32).astype(jnp.float32) + offset

    def add_mode(mode_number, summed):
        decay_col = lax.dynamic_slice_in_dim(decay, mode_number, 1, 1)
        weight_col = lax.dynamic_slice_in_dim(residue, mode_number, 1, 1)
        return summed + weight_col * jnp.exp(-decay_col * positions[None, :])

    return lax.fori_loop(
        0, decay.shape[1], add_mode, jnp.zeros((decay.shape[0], length), jnp.float32)
    )


def on_device(
    token_ids, embed_table, projected_table, feat_one, inner_taps, feat_two, decay, residue
):
    tok_rows = token_ids.shape[0]
    channels = embed_table.shape[1]
    lead_one = feat_one.shape[0] - 1 + inner_taps.shape[0] - 1
    lead_two = feat_two.shape[0] - 1
    embedded, raw_rows = look_up(token_ids, embed_table, projected_table)
    raw_sent = raw_rows[tok_rows - lead_one :].astype(jnp.bfloat16)
    earlier = shifted(raw_sent, "ctx", 1)
    raw_ext = jnp.concatenate([earlier.astype(jnp.float32), raw_rows], axis=0)
    stream = block_one(raw_ext, embedded, feat_one, inner_taps)
    before = shifted(stream[tok_rows - lead_two :], "ctx", 1)
    stream_ext = jnp.concatenate([before, stream], axis=0)
    widened = stream_ext.astype(jnp.float32)
    squares = lax.psum(jnp.sum(widened * widened, axis=1), "tp")
    normed = widened * lax.rsqrt(squares / D + epsilon)[:, None]
    queries = valid_taps(normed, feat_two[:, 0])
    key_rows = valid_taps(normed, feat_two[:, 1])
    valued = valid_taps(normed, feat_two[:, 2])
    product = jnp.transpose(key_rows * valued).astype(jnp.bfloat16)
    per_device = channels // lax.axis_size("ctx")
    gathered = lax.all_to_all(product, "ctx", split_axis=0, concat_axis=1, tiled=True)
    first_lane = lax.axis_index("ctx") * per_device
    my_decay = lax.dynamic_slice_in_dim(decay, first_lane, per_device, 0)
    my_residue = lax.dynamic_slice_in_dim(residue, first_lane, per_device, 0)
    response = mode_response(my_decay, my_residue, gathered.shape[1], 0.0)
    convolved = causal_convolve(gathered, response)
    carried = lax.all_to_all(convolved, "ctx", split_axis=1, concat_axis=0, tiled=True)
    mixed_out = queries * jnp.transpose(carried)
    return (widened[lead_two:] + mixed_out).astype(jnp.bfloat16)


def solution(mesh):
    placed = (
        P("ctx"),
        P(None, "tp"),
        P(None, None, "tp"),
        P(None, None, "tp"),
        P(None, "tp"),
        P(None, None, "tp"),
        P("tp", None),
        P("tp", None),
    )
    return jax.shard_map(
        on_device, mesh=mesh, in_specs=placed, out_specs=P("ctx", "tp"), check_vma=False
    )
```

profile of v0, /device:TPU:15, one launch (start us, length us, event | category | flops | bytes accessed | tf_op | source)
XLA Modules:
  0.0 1082.3 jit_solution(17847357074202862382)
XLA Ops:
  0.0 16.6 %copy.72 = bf16[512,3,4096]{0,2,1:T(8,128)(2,1)} copy(bf16[512,3,4096]{2,0,1:T(8,128)(2,1)} %param.12) | data formatting | bytes 25165824 | tf_op args[2]
  16.7 20.7 %fusion.72 = f32[512,12288]{1,0:T(8,128)} fusion(bf16[512,12288]{0,1:T(8,128)(2,1)} %bitcast.240, s32[512]{0:T(512)S(1)} %copy-done.9), kind=kOutput, calls=%fused_computation.119 | convolution fusion | flops 6442713088 | bytes 37750784 | tf_op jit(solution)/shard_map/dot_general | solution.py:40
  37.4 1.0 slice.538
  38.4 3.7 collective-permute-start
  44.1 100.5 %while.14 = (s32[]{:T(128)}, f32[256,8192]{1,0:T(8,128)}, f32[256,16]{0,1:T(8,128)S(1)}, f32[256,16]{0,1:T(8,128)S(1)}, s32[]{:T(128)}, /*index=5*/s32[]{:T(128)}) while((s32[]{:T(128)}, f32[256,8192]{1,0:T(8,128)}, f32[256,16]{0,1:T(8,128)S(1)}, f32[256,16]{0,1:T(8,128)S(1)}, s32[]{:T(128)}, /*index=5*/s32[]{:T(128)}) %tuple.64), condition=%wide.region_3.0_spmd.clone, body=%wide.region_2.0_spmd.clone.sunk | while | flops 8397059 | bytes 16848984 | solution.py:149
  44.6 4.2 select_add_fusion.2
  48.9 6.4 select_add_fusion.2
  55.2 6.4 select_add_fusion.2
  61.6 6.4 select_add_fusion.2
  68.0 6.4 select_add_fusion.2
  74.4 6.4 select_add_fusion.2
  80.8 6.4 select_add_fusion.2
  87.2 6.4 select_add_fusion.2
  93.5 6.4 select_add_fusion.2
  99.9 6.4 select_add_fusion.2
  106.3 6.4 select_add_fusion.2
  112.7 6.4 select_add_fusion.2
  119.1 6.4 select_add_fusion.2
  125.5 6.4 select_add_fusion.2
  131.9 6.4 select_add_fusion.2
  138.2 6.4 select_add_fusion.2
  144.6 5.0 copy.153
  149.6 3.3 copy-done.3
  152.9 29.2 %fusion.100 = f32[256,128,128]{2,1,0:T(8,128)} fusion(f32[256,64,128]{2,1,0:T(8,128)S(1)} %bitcast.238, f32[128,128]{0,1:T(8,128)S(1)} %sine_negate_fusion.1), kind=kOutput, calls=%fused_computation.158 | convolution fusion | flops 3221225472 | bytes 25198592 | tf_op jit(solution)/shard_map/kp,bpq->bkq/dot_general | solution.py:91
  182.1 24.7 %copy.73 = f32[512,12288]{0,1:T(8,128)} copy(f32[512,12288]{1,0:T(8,128)} %fusion.72) | data formatting | bytes 50331648 | tf_op jit(solution)/shard_map/dot_general | solution.py:40
  206.8 25.0 %copy.74 = f32[512,3,4096]{2,0,1:T(8,128)} copy(f32[512,3,4096]{0,2,1:T(8,128)} %bitcast.241) | data formatting | bytes 50331648 | tf_op jit(solution)/shard_map/reshape | solution.py:41
  231.8 18.4 %fusion.21 = (f32[518,4096]{1,0:T(8,128)}, f32[518,4096]{1,0:T(8,128)}, f32[518,4096]{1,0:T(8,128)}) fusion(f32[512,3,4096]{2,0,1:T(8,128)} %copy.74, f32[8,3,4096]{2,0,1:T(8,128)S(1)} %convert_element_type.123), kind=kLoop, calls=%fused_computation.58 | loop fusion | flops 6365184 | bytes 51019776 | tf_op jit(solution)/shard_map/slice | solution.py:24
  250.2 21.3 %fusion.19 = f32[518,4096]{1,0:T(8,128)} fusion(f32[512,3,4096]{2,0,1:T(8,128)} %copy.74, f32[8,3,4096]{2,0,1:T(8,128)S(1)} %convert_element_type.123, f32[4096]{0:T(1024)S(1)} %bitcast.253, f32[4096]{0:T(1024)S(1)} %bitcast.254, f32[4096]{0:T(1024)S(1)} %bitcast.249, f32[4096]{0:T(1024)S(1)} %bitcast.250, f32[4096]{0:T(1024)S(1)} %bitcast.251, ...), kind=kLoop, calls=%fused_computation.56 | loop fusion | flops 36069376 | bytes 34144256 | tf_op jit(solution)/shard_map/mul | solution.py:48
  271.5 36.9 %fusion.46 = bf16[512,4096]{1,0:T(8,128)(2,1)} fusion(f32[518,4096]{1,0:T(8,128)} %fusion.19, f32[518,4096]{1,0:T(8,128)} %get-tuple-element.130, f32[518,4096]{1,0:T(8,128)} %get-tuple-element.131, f32[518,4096]{1,0:T(8,128)} %get-tuple-element.129, bf16[512,4096]{1,0:T(8,128)(2,1)} %param.11, f32[4096]{0:T(1024)S(1)} %bitcast.272, ...), kind=kOutput, calls=%fused_computation.87 | convolution fusion | flops 2191785984 | bytes 92440576 | tf_op jit(solution)/shard_map/dot_general | solution.py:38
  308.4 0.9 slice.343
  309.3 1.9 collective-permute-start.1
  311.5 0.9 collective-permute-done.1
  312.4 4.1 multiply_reduce_fusion
  316.5 3.8 psum.7
  320.3 3.7 broadcast_multiply_fusion
  324.0 4.5 multiply_convert_fusion
  328.5 2.4 copy.155
  330.9 7.8 all-to-all-start
  339.0 30.5 %fusion.102 = f32[256,128,128]{2,1,0:T(8,128)} fusion(f32[256,64,128]{2,1,0:T(8,128)} %bitcast.239, f32[128,128]{0,1:T(8,128)S(1)} %fusion.105), kind=kOutput, calls=%fused_computation.160 | convolution fusion | flops 3221225472 | bytes 25198592 | tf_op jit(solution)/shard_map/kp,bpq->bkq/dot_general | solution.py:91
  369.5 32.9 %fusion.66 = f32[256,128,128]{2,1,0:T(8,128)} fusion(f32[256,128,128]{2,1,0:T(8,128)S(1)} %bitcast.236, f32[256,128,128]{2,1,0:T(8,128)} %fusion.102, f32[128,128]{0,1:T(8,128)S(1)} %get-tuple-element.159, f32[128,128]{0,1:T(8,128)S(1)} %get-tuple-element.160), kind=kOutput, calls=%fused_computation.113 | convolution fusion | flops 6455279616 | bytes 50462720 | tf_op jit(solution)/shard_map/bkq,ql->bkl/dot_general | solution.py:104
  402.4 33.1 %fusion.68 = f32[256,128,128]{2,1,0:T(8,128)} fusion(f32[256,128,128]{2,1,0:T(8,128)S(1)} %bitcast.236, f32[256,128,128]{2,1,0:T(8,128)} %fusion.102, f32[128,128]{0,1:T(8,128)S(1)} %get-tuple-element.159, f32[128,128]{0,1:T(8,128)S(1)} %get-tuple-element.160), kind=kOutput, calls=%fused_computation.114 | convolution fusion | flops 6455263232 | bytes 50462720 | tf_op jit(solution)/shard_map/bkq,ql->bkl/dot_general | solution.py:101
  435.5 34.1 %convolution_add_fusion.3 = f32[256,128,128]{2,1,0:T(8,128)} fusion(f32[256,128,128]{2,1,0:T(8,128)} %fusion.66, f32[256,128,128]{2,1,0:T(8,128)S(1)} %bitcast.236, f32[256,128,128]{2,1,0:T(8,128)} %fusion.102, f32[128,128]{0,1:T(8,128)S(1)} %get-tuple-element.159, f32[128,128]{0,1:T(8,128)S(1)} %get-tuple-element.160), kind=kOutput, calls=%fused_computation.47 | convolution fusion | flops 6459457536 | bytes 67239936 | tf_op jit(solution)/shard_map/bkq,ql->bkl/dot_general | solution.py:104
  469.6 34.1 %convolution_subtract_fusion.1 = f32[256,128,128]{2,1,0:T(8,128)} fusion(f32[256,128,128]{2,1,0:T(8,128)} %fusion.68, f32[256,128,128]{2,1,0:T(8,128)S(1)} %bitcast.236, f32[256,128,128]{2,1,0:T(8,128)} %fusion.102, f32[128,128]{0,1:T(8,128)S(1)} %get-tuple-element.159, f32[128,128]{0,1:T(8,128)S(1)} %get-tuple-element.160), kind=kOutput, calls=%fused_computation.49 | convolution fusion | flops 6459473920 | bytes 67239936 | tf_op jit(solution)/shard_map/bkq,ql->bkl/dot_general | solution.py:101
  503.7 6.6 copy.135
  510.3 10.5 fusion.118
  520.8 7.4 fusion.120
  528.2 9.5 convolution_add_fusion
  537.7 21.2 %convolution_add_fusion.1 = f32[256,128,128]{2,1,0:T(8,128)} fusion(f32[256,128,128]{2,1,0:T(8,128)} %fusion.120, bf16[256,64,128]{2,1,0:T(8,128)(2,1)} %copy.135, f32[128,128]{0,1:T(8,128)S(1)} %fusion.105), kind=kOutput, calls=%fused_computation.44 | convolution fusion | flops 541097984 | bytes 37781504 | tf_op jit(solution)/shard_map/kp,bpq->bkq/dot_general | solution.py:90
  558.9 32.6 %fusion.60 = f32[256,128,128]{2,1,0:T(8,128)} fusion(f32[256,128,128]{2,1,0:T(8,128)S(1)} %convolution_add_fusion, f32[256,128,128]{2,1,0:T(8,128)} %convolution_add_fusion.1, f32[128,128]{0,1:T(8,128)S(1)} %get-tuple-element.159, f32[128,128]{0,1:T(8,128)S(1)} %get-tuple-element.160), kind=kOutput, calls=%fused_computation.111 | convolution fusion | flops 6455279616 | bytes 50462720 | tf_op jit(solution)/shard_map/bkq,ql->bkl/dot_general | solution.py:104
  591.5 32.8 %fusion.62 = f32[256,128,128]{2,1,0:T(8,128)} fusion(f32[256,128,128]{2,1,0:T(8,128)S(1)} %convolution_add_fusion, f32[256,128,128]{2,1,0:T(8,128)} %convolution_add_fusion.1, f32[128,128]{0,1:T(8,128)S(1)} %get-tuple-element.159, f32[128,128]{0,1:T(8,128)S(1)} %get-tuple-element.160), kind=kOutput, calls=%fused_computation.112 | convolution fusion | flops 6455263232 | bytes 50462720 | tf_op jit(solution)/shard_map/bkq,ql->bkl/dot_general | solution.py:101
  624.3 34.1 %convolution_subtract_fusion.2 = f32[256,128,128]{2,1,0:T(8,128)} fusion(f32[256,128,128]{2,1,0:T(8,128)} %fusion.62, f32[256,128,128]{2,1,0:T(8,128)S(1)} %convolution_add_fusion, f32[256,128,128]{2,1,0:T(8,128)} %convolution_add_fusion.1, f32[128,128]{0,1:T(8,128)S(1)} %get-tuple-element.159, f32[128,128]{0,1:T(8,128)S(1)} %get-tuple-element.160), kind=kOutput, calls=%fused_computation.50 | convolution fusion | flops 6459473920 | bytes 67239936 | tf_op jit(solution)/shard_map/bkq,ql->bkl/dot_general | solution.py:101
  658.4 51.1 %multiply_add_fusion = (f32[256,128,128]{2,1,0:T(8,128)}, f32[256,128,128]{2,1,0:T(8,128)}) fusion(f32[256,128,128]{2,1,0:T(8,128)} %convolution_subtract_fusion.1, f32[256,128,128]{2,1,0:T(8,128)} %convolution_subtract_fusion.2, f32[256,128,128]{2,1,0:T(8,128)} %convolution_add_fusion.3, f32[256,128,128]{2,1,0:T(8,128)} %fusion.60, ...), kind=kOutput, calls=%fused_computation.33 | convolution fusion | flops 6484623360 | bytes 134348800 | tf_op jit(solution)/shard_map/bkq,ql->bkl/dot_general | solution.py:104
  709.4 23.2 %fusion.85 = f32[256,128,128]{1,2,0:T(8,128)} fusion(f32[256,128,128]{2,1,0:T(8,128)} %get-tuple-element.127), kind=kOutput, calls=%fused_computation.140 | convolution fusion | flops 6442680320 | bytes 33554432 | tf_op jit(solution)/shard_map/bkl,lq->bkq/dot_general | solution.py:118
  732.7 22.9 %fusion.87 = f32[256,128,128]{1,2,0:T(8,128)} fusion(f32[256,128,128]{2,1,0:T(8,128)} %get-tuple-element.128), kind=kOutput, calls=%fused_computation.142 | convolution fusion | flops 6442680320 | bytes 33554432 | tf_op jit(solution)/shard_map/bkl,lq->bkq/dot_general | solution.py:115
  755.6 24.0 %convolution_subtract_fusion = f32[256,128,128]{1,2,0:T(8,128)} fusion(f32[256,128,128]{1,2,0:T(8,128)} %fusion.85, f32[256,128,128]{2,1,0:T(8,128)} %get-tuple-element.128), kind=kOutput, calls=%fused_computation.45 | convolution fusion | flops 6446891008 | bytes 50331648 | tf_op jit(solution)/shard_map/bkl,lq->bkq/dot_general | solution.py:118
  779.6 23.9 %convolution_add_fusion.2 = f32[256,128,128]{1,2,0:T(8,128)} fusion(f32[256,128,128]{1,2,0:T(8,128)} %fusion.87, f32[256,128,128]{2,1,0:T(8,128)} %get-tuple-element.127), kind=kOutput, calls=%fused_computation.46 | convolution fusion | flops 6446891008 | bytes 50331648 | tf_op jit(solution)/shard_map/bkl,lq->bkq/dot_general | solution.py:115
  803.4 28.4 %fusion.6 = f32[256,128,64]{1,2,0:T(8,128)} fusion(f32[256,128,128]{1,2,0:T(8,128)} %convolution_add_fusion.2, f32[256,128,128]{1,2,0:T(8,128)} %convolution_subtract_fusion, f32[128,128]{0,1:T(8,128)S(1)} %get-tuple-element.159, f32[128,128]{0,1:T(8,128)S(1)} %get-tuple-element.160, f32[128,128]{0,1:T(8,128)S(1)} %copy-done.6), kind=kOutput, calls=%fused_computation.25 | convolution fusion | flops 3233808384 | bytes 42139648 | tf_op jit(solution)/shard_map/pk,bkq->bpq/dot_general | solution.py:125
  831.9 26.7 %multiply_bitcast_fusion = f32[256,64,128]{2,1,0:T(8,128)} fusion(f32[256,128,64]{1,2,0:T(8,128)} %fusion.6, f32[256,128,128]{1,2,0:T(8,128)} %convolution_subtract_fusion, f32[256,128,128]{1,2,0:T(8,128)} %convolution_add_fusion.2, f32[128,128]{0,1:T(8,128)S(1)} %get-tuple-element.159, f32[128,128]{0,1:T(8,128)S(1)} %get-tuple-element.160, ...), kind=kOutput, calls=%fused_computation.105 | convolution fusion | flops 3238002688 | bytes 50528256 | tf_op jit(solution)/shard_map/pk,bkq->bpq/dot_general | solution.py:123
  858.6 9.2 copy.150
  867.8 6.1 all-to-all-start.1
  873.9 6.8 maximum_convert_fusion
  880.7 175.6 %all-to-all-done.1 = f32[256,16,512]{0,2,1:T(8,128)} async-done(((f32[256,16,512]{0,2,1:T(8,128)}), f32[256,16,512]{0,2,1:T(8,128)}, u32[]{:S(2)}, u32[]{:S(2)}) %all-to-all-start.1) | async-done | bytes 8388640 | tf_op jit(solution)/shard_map/all_to_all | solution.py:182
  1056.3 7.9 copy.152
  1064.2 17.9 %fusion.42 = bf16[512,4096]{1,0:T(8,128)(2,1)} fusion(f32[514,4096]{1,0:T(8,128)} %maximum_convert_fusion, f32[4096,512]{0,1:T(8,128)} %bitcast.243, f32[514,4096]{1,0:T(8,128)} %copy-done.1, f32[4096]{0:T(1024)S(1)} %bitcast.256, f32[4096]{0:T(1024)S(1)} %bitcast.257, f32[4096]{0:T(1024)S(1)} %bitcast.255), kind=kLoop, calls=%fused_computation.82 | loop fusion | flops 16777216 | bytes 46186496 | tf_op jit(solution)/shard_map/convert_element_type | solution.py:184
  (88 shorter events, 2.8 us)
Async XLA Ops:
  0.0 16.6 %copy-start.9 = (s32[512]{0:T(512)S(1)}, s32[512]{0:T(512)}, u32[]{:S(2)}) copy-start(s32[512]{0:T(512)} %param.10) | copy-start | bytes 6148
  16.6 25.8 %copy-start.14 = (f32[7,4096]{1,0:T(8,128)S(1)}, f32[7,4096]{1,0:T(8,128)}, u32[]{:S(2)}) copy-start(f32[7,4096]{1,0:T(8,128)} %param.14) | copy-start | bytes 344068
  16.6 25.9 %copy-start.12 = (f32[3,3,4096]{2,1,0:T(4,128)S(1)}, f32[3,3,4096]{2,1,0:T(4,128)}, u32[]{:S(2)}) copy-start(f32[3,3,4096]{2,1,0:T(4,128)} %param.13) | copy-start | bytes 442372
  16.7 26.0 %copy-start.13 = (f32[3,3,4096]{2,1,0:T(4,128)S(1)}, f32[3,3,4096]{2,1,0:T(4,128)}, u32[]{:S(2)}) copy-start(f32[3,3,4096]{2,1,0:T(4,128)} %param.15) | copy-start | bytes 442372
  38.4 193.4 %collective-permute-start = (bf16[8,3,4096]{2,0,1:T(8,128)(2,1)S(1)}, bf16[8,3,4096]{2,0,1:T(8,128)(2,1)S(1)}, u32[]{:S(2)}, u32[]{:S(2)}) collective-permute-start(bf16[8,3,4096]{2,0,1:T(8,128)(2,1)S(1)} %bitcast.246), channel_id=1, source_target_pairs={{0,2},{2,4},{4,6},{6,8},{8,10},{10,12},{12,14},{14,16},{16,18},{18... | collective-permute-start | bytes 589832 | tf_op jit(solution)/shard_map/ppermute | solution.py:18
  42.4 107.2 %copy-start.4 = (f32[128,128]{0,1:T(8,128)}, f32[128,128]{0,1:T(8,128)S(1)}, u32[]{:S(2)}) copy-start(f32[128,128]{0,1:T(8,128)S(1)} %sine_negate_fusion.1) | copy-start | bytes 196612
  149.6 3.3 copy-start.3
  309.3 3.1 collective-permute-start.1
  312.4 16.1 %copy-start.10 = (bf16[2,4096]{1,0:T(2,128)(2,1)}, bf16[2,4096]{1,0:T(2,128)(2,1)S(1)}, u32[]{:S(2)}) copy-start(bf16[2,4096]{1,0:T(2,128)(2,1)S(1)} %collective-permute-done.1) | copy-start | bytes 49156
  324.0 4.5 copy-start.1
  330.9 172.8 %all-to-all-start = ((bf16[16,256,512]{1,2,0:T(8,128)(2,1)}), bf16[16,256,512]{1,2,0:T(8,128)(2,1)}, u32[]{:S(2)}, u32[]{:S(2)}) async-start(bf16[16,256,512]{1,2,0:T(8,128)(2,1)} %bitcast.244), calls=%async_computation | async-start | bytes 8388608 | tf_op jit(solution)/shard_map/all_to_all | solution.py:176
  338.7 30.8 %slice-start = ((s8[16777216]{0:T(1024)(128)(4,1)}), s8[4194304]{0:T(1024)(128)(4,1)S(1)}, s32[]{:S(2)}) async-start(s8[16777216]{0:T(1024)(128)(4,1)} %bitcast.235), calls=%async_computation.2 | async-start | bytes 8388608
  339.0 198.7 %copy-start.7 = (f32[128,128]{0,1:T(8,128)}, f32[128,128]{0,1:T(8,128)S(1)}, u32[]{:S(2)}) copy-start(f32[128,128]{0,1:T(8,128)S(1)} %fusion.105) | copy-start | bytes 196612
  339.0 30.5 %slice-start.1 = ((s8[16777216]{0:T(1024)(128)(4,1)}), s8[4194304]{0:T(1024)(128)(4,1)S(1)}, s32[]{:S(2)}) async-start(s8[16777216]{0:T(1024)(128)(4,1)} %bitcast.235), calls=%async_computation.3 | async-start | bytes 8388608
  339.0 30.5 %slice-start.2 = ((s8[16777216]{0:T(1024)(128)(4,1)}), s8[4194304]{0:T(1024)(128)(4,1)S(1)}, s32[]{:S(2)}) async-start(s8[16777216]{0:T(1024)(128)(4,1)} %bitcast.235), calls=%async_computation.4 | async-start | bytes 8388608
  339.0 30.5 %slice-start.3 = ((s8[16777216]{0:T(1024)(128)(4,1)}), s8[4194304]{0:T(1024)(128)(4,1)S(1)}, s32[]{:S(2)}) async-start(s8[16777216]{0:T(1024)(128)(4,1)} %bitcast.235), calls=%async_computation.5 | async-start | bytes 8388608
  469.6 40.7 %copy-start.5 = (f32[128,128]{0,1:T(8,128)S(1)}, f32[128,128]{0,1:T(8,128)}, u32[]{:S(2)}) copy-start(f32[128,128]{0,1:T(8,128)} %copy-done.4) | copy-start | bytes 196612
  510.3 10.5 copy-start.2
  537.7 86.6 %copy-start = (f32[256,128,128]{2,1,0:T(8,128)}, f32[256,128,128]{2,1,0:T(8,128)S(1)}, u32[]{:S(2)}) copy-start(f32[256,128,128]{2,1,0:T(8,128)S(1)} %convolution_add_fusion) | copy-start | bytes 50331652
  779.6 23.9 %copy-start.6 = (f32[128,128]{0,1:T(8,128)S(1)}, f32[128,128]{0,1:T(8,128)}, u32[]{:S(2)}) copy-start(f32[128,128]{0,1:T(8,128)} %copy-done.4) | copy-start | bytes 196612
  803.4 28.4 %copy-start.8 = (f32[128,128]{0,1:T(8,128)S(1)}, f32[128,128]{0,1:T(8,128)}, u32[]{:S(2)}) copy-start(f32[128,128]{0,1:T(8,128)} %copy-done.7) | copy-start | bytes 196612
  867.8 6.2 copy-start.11
  867.8 188.5 %all-to-all-start.1 = ((f32[256,16,512]{0,2,1:T(8,128)}), f32[256,16,512]{0,2,1:T(8,128)}, u32[]{:S(2)}, u32[]{:S(2)}) async-start(f32[256,16,512]{0,2,1:T(8,128)} %bitcast.242), calls=%async_computation.1 | async-start | bytes 16777216 | tf_op jit(solution)/shard_map/all_to_all | solution.py:182
  880.7 183.4 %copy-start.15 = (f32[1,1,4096]{2,1,0:T(1,128)S(1)}, f32[1,1,4096]{2,1,0:T(1,128)}, u32[]{:S(2)}) copy-start(f32[1,1,4096]{2,1,0:T(1,128)} %get-tuple-element.132) | copy-start | bytes 49156
  880.7 183.4 %copy-start.16 = (f32[1,1,4096]{2,1,0:T(1,128)S(1)}, f32[1,1,4096]{2,1,0:T(1,128)}, u32[]{:S(2)}) copy-start(f32[1,1,4096]{2,1,0:T(1,128)} %get-tuple-element.137) | copy-start | bytes 49156
  880.7 183.4 %copy-start.17 = (f32[1,1,4096]{2,1,0:T(1,128)S(1)}, f32[1,1,4096]{2,1,0:T(1,128)}, u32[]{:S(2)}) copy-start(f32[1,1,4096]{2,1,0:T(1,128)} %get-tuple-element.138) | copy-start | bytes 49156
where the time goes:
time: 1090 us; the launch traced here: 1080 us
  matrix products  600 us (55%)
  other arithmetic  177 us (16%)
  waiting for transfers between devices  176 us (16%)
  local copies, waits for them, and re-layouts  104 us (10%)
  starting transfers between devices  19.6 us (2%)
    all_to_all x1, waiting for transfers between devices, on_device(): lax.all_to_all(convolved, 'ctx', split_axis=1, concat_axis=0, tiled=True)  176 us
    add x16, other arithmetic, add_mode(): return summed + weight_col * jnp.exp(-decay_col * positions[None, :])  99.6 us
    dot_general x2, matrix products, forward_transform(): jnp.einsum('bkq,ql->bkl', turned_im, col_re, precision=PRECISE)  85.2 us
    dot_general x2, matrix products, forward_transform(): jnp.einsum('bkq,ql->bkl', turned_im, col_im, precision=PRECISE)  68.2 us
    dot_general x2, matrix products, forward_transform(): jnp.einsum('bkq,ql->bkl', turned_re, col_re, precision=PRECISE)  65.9 us
    dot_general x2, matrix products, forward_transform(): jnp.einsum('bkq,ql->bkl', turned_re, col_im, precision=PRECISE)  65.4 us
    dot_general x2, matrix products, first_section(): return jnp.einsum('kp,bpq->bkq', table, signal, precision=PRECISE)  59.7 us
    dot_general x1, matrix products, look_up(): embedded = jnp.dot(one_hot, embed_table, preferred_element_type=jnp.float32)  36.9 us
  transfers between devices with their start and end apart: 4, of which 2 were waited for; matrix products, arithmetic and copies ran while one was open for 33% of the time, Pallas kernels for 0%

commit v1 on v0

v1 whole, which is shorter than its diff:
```python
import functools

import jax
import jax.numpy as jnp
from jax import lax
from jax.experimental import pallas as pl
from jax.experimental.pallas import tpu as pltpu
from jax.sharding import PartitionSpec as P

epsilon = 1e-06
HALO = 16
SEGMENTS = 8
LANES = 128
VMEM_LIMIT = 60 * 1024 * 1024


def shifted(value, axis, steps):
    count = lax.axis_size(axis)
    return lax.ppermute(value, axis, [(source, source + steps) for source in range(count - steps)])


def rolled_taps(series, taps):
    summed = taps[0] * series
    for offset in range(1, len(taps)):
        summed = summed + taps[offset] * pltpu.roll(series, offset, 0)
    return summed


def block_rows(rows):
    chunk = 128 if (rows - HALO) % 128 == 0 else rows - HALO
    spans = [(0, 0, HALO)]
    spans += [(start - HALO, start, chunk) for start in range(HALO, rows, chunk)]
    return spans


def first_kernel(one_hot, embed, proj, feat, inner, stream, squares, raw):
    rows = one_hot.shape[0]
    width = embed.shape[1]
    ids = one_hot[...]
    raw[0] = jnp.dot(ids, embed[...], preferred_element_type=jnp.float32)
    for s in range(3):
        raw[1 + s] = jnp.dot(ids, proj[s], preferred_element_type=jnp.float32)

    @pl.when(pl.program_id(0) == 0)
    def _():
        squares[...] = jnp.zeros_like(squares)

    @pl.loop(0, width // LANES)
    def _(block):
        lanes = pl.ds(pl.multiple_of(block * LANES, LANES), LANES)
        feat_taps = [[feat[j, s : s + 1, lanes] for j in range(feat.shape[0])] for s in range(3)]
        inner_taps = [inner[j : j + 1, lanes] for j in range(inner.shape[0])]
        for base, start, count in block_rows(rows):
            slab = pl.ds(base, start - base + count)
            queries = rolled_taps(raw[1, slab, lanes], feat_taps[0])
            keyed = rolled_taps(raw[2, slab, lanes], feat_taps[1])
            valued = rolled_taps(raw[3, slab, lanes], feat_taps[2])
            mixture = rolled_taps(keyed * valued, inner_taps)
            total = (raw[0, slab, lanes] + queries * mixture)[start - base :].astype(jnp.bfloat16)
            stream[pl.ds(start, count), lanes] = total
            wide = total.astype(jnp.float32)
            squares[pl.ds(start, count), :] += wide * wide


def second_kernel(stream, inverse, feat, rate, product, states, series):
    rows = stream.shape[0]
    width = stream.shape[1]
    steps = (rows - HALO) // SEGMENTS
    modes = rate.shape[0]
    for block in range(width // LANES):
        lanes = slice(block * LANES, (block + 1) * LANES)
        taps = [[feat[j, s : s + 1, lanes] for j in range(feat.shape[0])] for s in (1, 2)]
        for base, start, count in block_rows(rows)[1:]:
            slab = pl.ds(base, start - base + count)
            normed = stream[slab, lanes].astype(jnp.float32) * inverse[slab, :]
            both = rolled_taps(normed, taps[0]) * rolled_taps(normed, taps[1])
            rounded = both[start - base :].astype(jnp.bfloat16)
            product[pl.ds(start - HALO, count), lanes] = rounded
            series[block, pl.ds(start - HALO, count), :] = rounded.astype(jnp.float32)
        rates = [jnp.broadcast_to(rate[m : m + 1, lanes], (SEGMENTS, LANES)) for m in range(modes)]

        def step(at, held):
            value = series[block, pl.ds(at, SEGMENTS, stride=steps), :]
            return tuple(rates[m] * held[m] + value for m in range(modes))

        zero = jnp.zeros((SEGMENTS, LANES), jnp.float32)
        held = lax.fori_loop(0, steps, step, (zero,) * modes, unroll=4)
        for m in range(modes):
            states[m, :, lanes] = held[m]


def third_kernel(stream, inverse, feat, rate, weight, product, states, out, series, result):
    rows = stream.shape[0]
    width = stream.shape[1]
    steps = (rows - HALO) // SEGMENTS
    modes = rate.shape[0]
    for block in range(width // LANES):
        lanes = slice(block * LANES, (block + 1) * LANES)
        series[block] = product[:, lanes].astype(jnp.float32)
        rates = [jnp.broadcast_to(rate[m : m + 1, lanes], (SEGMENTS, LANES)) for m in range(modes)]
        weights = [
            jnp.broadcast_to(weight[m : m + 1, lanes], (SEGMENTS, LANES)) for m in range(modes)
        ]

        def step(at, held):
            where = pl.ds(at, SEGMENTS, stride=steps)
            value = series[block, where, :]
            held = tuple(rates[m] * held[m] + value for m in range(modes))
            terms = [weights[m] * held[m] for m in range(modes)]
            while len(terms) > 1:
                pairs = [a + b for a, b in zip(terms[::2], terms[1::2])]
                terms = pairs + terms[2 * len(pairs) :]
            result[block, where, :] = terms[0]
            return held

        first = tuple(states[m, :, lanes] for m in range(modes))
        lax.fori_loop(0, steps, step, first, unroll=4)
        taps = [feat[j, 0:1, lanes] for j in range(feat.shape[0])]
        for base, start, count in block_rows(rows)[1:]:
            slab = pl.ds(base, start - base + count)
            wide = stream[slab, lanes].astype(jnp.float32)
            queries = rolled_taps(wide * inverse[slab, :], taps)[start - base :]
            convolved = result[block, pl.ds(start - HALO, count), :]
            total = wide[start - base :] + queries * convolved
            out[pl.ds(start - HALO, count), lanes] = total.astype(jnp.bfloat16)


def on_device(
    token_ids, embed_table, projected_table, feat_one, inner_taps, feat_two, decay, residue
):
    tokens = token_ids.shape[0]
    vocab, channels = embed_table.shape
    modes = decay.shape[1]
    rows = tokens + HALO
    count = lax.axis_size("ctx")
    all_channels = channels * lax.axis_size("tp")
    params = pltpu.CompilerParams(
        dimension_semantics=("arbitrary",), vmem_limit_bytes=VMEM_LIMIT
    )

    earlier = shifted(token_ids[tokens - HALO :] + 1, "ctx", 1) - 1
    ids = jnp.concatenate([earlier, token_ids])
    one_hot = (ids[:, None] == jnp.arange(vocab, dtype=jnp.int32)[None, :]).astype(jnp.bfloat16)
    proj = jnp.transpose(projected_table, (1, 0, 2))

    wide = min(512, channels)
    feat_spec = lambda size: pl.BlockSpec((feat_one.shape[0], 3, size), lambda c: (0, 0, c))
    stream, squares = pl.pallas_call(
        first_kernel,
        grid=(channels // wide,),
        in_specs=[
            pl.BlockSpec((rows, vocab), lambda c: (0, 0)),
            pl.BlockSpec((vocab, wide), lambda c: (0, c)),
            pl.BlockSpec((3, vocab, wide), lambda c: (0, 0, c)),
            feat_spec(wide),
            pl.BlockSpec((inner_taps.shape[0], wide), lambda c: (0, c)),
        ],
        out_specs=[
            pl.BlockSpec((rows, wide), lambda c: (0, c)),
            pl.BlockSpec((rows, LANES), lambda c: (0, 0)),
        ],
        out_shape=[
            jax.ShapeDtypeStruct((rows, channels), jnp.bfloat16),
            jax.ShapeDtypeStruct((rows, LANES), jnp.float32),
        ],
        scratch_shapes=[pltpu.VMEM((4, rows, wide), jnp.float32)],
        compiler_params=params,
        name="first_block",
    )(one_hot, embed_table, proj, feat_one, inner_taps)

    summed = lax.psum(jnp.sum(squares, axis=1), "tp")
    inverse = lax.rsqrt(summed / all_channels + epsilon)
    inverse = jnp.broadcast_to(inverse[:, None], (rows, LANES))

    slope = jnp.transpose(decay)
    weight = jnp.transpose(residue)
    rate = jnp.exp(-slope)
    size = min(256, channels)
    blocks = size // LANES
    stream_spec = pl.BlockSpec((rows, size), lambda c: (0, c))
    inverse_spec = pl.BlockSpec((rows, LANES), lambda c: (0, 0))
    mode_spec = pl.BlockSpec((modes, size), lambda c: (0, c))
    token_spec = pl.BlockSpec((tokens, size), lambda c: (0, c))
    state_spec = pl.BlockSpec((modes, SEGMENTS, size), lambda c: (0, 0, c))
    product, states = pl.pallas_call(
        second_kernel,
        grid=(channels // size,),
        in_specs=[stream_spec, inverse_spec, feat_spec(size), mode_spec],
        out_specs=[token_spec, state_spec],
        out_shape=[
            jax.ShapeDtypeStruct((tokens, channels), jnp.bfloat16),
            jax.ShapeDtypeStruct((modes, SEGMENTS, channels), jnp.float32),
        ],
        scratch_shapes=[pltpu.VMEM((blocks, tokens, LANES), jnp.float32)],
        compiler_params=params,
        name="local_states",
    )(stream, inverse, feat_two, rate)

    per_segment = jnp.exp(-slope * float(tokens // SEGMENTS))
    whole = states[:, 0]
    for s in range(1, SEGMENTS):
        whole = per_segment * whole + states[:, s]
    spread = lax.all_to_all(whole, "ctx", split_axis=1, concat_axis=0, tiled=True)
    spread = spread.reshape(count, modes, channels // count)
    share = channels // count
    mine = lax.dynamic_slice_in_dim(slope, lax.axis_index("ctx") * share, share, 1)
    per_shard = jnp.exp(-mine * float(tokens))
    carry = jnp.zeros((modes, share), jnp.float32)
    carries = []
    for s in range(count):
        carries.append(carry)
        carry = per_shard * carry + spread[s]
    carried = jnp.concatenate(carries, axis=0)
    start = lax.all_to_all(carried, "ctx", split_axis=0, concat_axis=1, tiled=True)
    starts = [start]
    for s in range(SEGMENTS - 1):
        starts.append(per_segment * starts[-1] + states[:, s])
    entering = jnp.stack(starts, axis=1)

    return pl.pallas_call(
        third_kernel,
        grid=(channels // size,),
        in_specs=[
            stream_spec,
            inverse_spec,
            feat_spec(size),
            mode_spec,
            mode_spec,
            token_spec,
            state_spec,
        ],
        out_specs=token_spec,
        out_shape=jax.ShapeDtypeStruct((tokens, channels), jnp.bfloat16),
        scratch_shapes=[
            pltpu.VMEM((blocks, tokens, LANES), jnp.float32),
            pltpu.VMEM((blocks, tokens, LANES), jnp.float32),
        ],
        compiler_params=params,
        name="long_convolution",
    )(stream, inverse, feat_two, rate, weight, product, entering)


def solution(mesh):
    placed = (
        P("ctx"),
        P(None, "tp"),
        P(None, None, "tp"),
        P(None, None, "tp"),
        P(None, "tp"),
        P(None, None, "tp"),
        P("tp", None),
        P("tp", None),
    )
    return jax.shard_map(
        on_device, mesh=mesh, in_specs=placed, out_specs=P("ctx", "tp"), check_vma=False
    )
```

time: 1090 us -> 144 us (0.13)
  the two profiles are of different devices: /device:TPU:15 before, /device:TPU:0 now
where the time goes in v1:
time: 144 us
  Pallas kernels  87.6 us (61%)
  blocking collectives  17.9 us (12%)
  local copies, waits for them, and re-layouts  11.5 us (8%)
  starting transfers between devices  10.3 us (7%)
  waiting for transfers between devices  10 us (7%)
  other arithmetic  6.05 us (4%)
    pallas_call x1, Pallas kernels, on_device(): pl.pallas_call(third_kernel, grid=(channels // size,), in_specs=[stream_s...  33.7 us
    pallas_call x1, Pallas kernels, on_device(): pl.pallas_call(first_kernel, grid=(channels // wide,), in_specs=[pl.Block...  31.1 us
    pallas_call x1, Pallas kernels, on_device(): pl.pallas_call(second_kernel, grid=(channels // size,), in_specs=[stream_...  22.9 us
    all_to_all x1, blocking collectives, on_device(): lax.all_to_all(carried, 'ctx', split_axis=0, concat_axis=1, tiled=True)  12.7 us
    all_to_all x1, waiting for transfers between devices, on_device(): lax.all_to_all(whole, 'ctx', split_axis=1, concat_axis=0, tiled=True)  10 us
    all_to_all x1, starting transfers between devices, on_device(): lax.all_to_all(whole, 'ctx', split_axis=1, concat_axis=0, tiled=True)  7.87 us
    another operation x9, local copies, waits for them, and re-layouts, on_device(): entering = jnp.stack(starts, axis=1)  6.9 us
    psum x1, blocking collectives, on_device(): summed = lax.psum(jnp.sum(squares, axis=1), 'tp')  5.24 us
  transfers between devices with their start and end apart: 2, of which 1 were waited for; matrix products, arithmetic and copies ran while one was open for 1% of the time, Pallas kernels for 0%

profile of v1, /device:TPU:0, one launch (start us, length us, event | category | flops | bytes accessed | tf_op | source)
XLA Modules:
  0.0 143.6 jit_solution(4237476512032317427)
XLA Ops:
  0.0 0.8 slice_add_fusion
  0.8 2.4 %collective-permute-start = (s32[16]{0:T(128)S(1)}, s32[16]{0:T(128)S(1)}, u32[]{:S(2)}, u32[]{:S(2)}) collective-permute-start(s32[16]{0:T(128)S(1)} %slice_add_fusion), channel_id=1, source_target_pairs={{0,2},{2,4},{4,6},{6,8},{8,10},{10,12},{12,14},{14,16},{16,18},{18... | collective-permute-start | bytes 200 | tf_op jit(solution)/shard_map/ppermute | solution.py:19
  3.1 1.7 %exponential_bitcast_fusion.rate = f32[16,4096]{1,0:T(8,128)} fusion(f32[4096,16]{0,1:T(8,128)} %param.14), kind=kLoop, calls=%fused_computation.40 | loop fusion | flops 65536 | bytes 524288 | tf_op jit(solution)/shard_map/exp | solution.py:177
  4.8 0.0 collective-permute-done
  4.8 0.8 pad_add_fusion
  5.6 1.0 fusion.one_hot
  6.6 31.1 %first_block.1 = (bf16[528,4096]{1,0:T(8,128)(2,1)}, f32[528,128]{1,0:T(8,128)}) custom-call(bf16[528,512]{1,0:T(8,128)(2,1)} %fusion.one_hot, bf16[512,4096]{1,0:T(8,128)(2,1)} %embed.1, bf16[3,512,4096]{2,1,0:T(8,128)(2,1)} %bitcast.378, f32[3,3,4096]{2,1,0:T(4,128)} %feat.3, f32[7,4096]{1,0:T(8,128)} %inner.1), custom_call_target="tpu_custom_call" | custom-call | tf_op jit(solution)/shard_map/first_block/pallas_call | solution.py:148
  37.6 1.1 reduce_sum.9
  38.7 5.2 %psum.7 = f32[528]{0:T(1024)S(1)} all-reduce(f32[528]{0:T(1024)S(1)} %reduce_sum.9), channel_id=1, replica_groups=mesh['ctx'=16,'tp'=2] {'tp'}, use_global_device_ids=true, to_apply=%region_1.0 | all-reduce | flops 528 | bytes 4224 | tf_op jit(solution)/shard_map/psum | solution.py:171
  44.0 0.9 broadcast_in_dim.4.inverse
  44.9 22.9 %local_states.1 = (bf16[512,4096]{1,0:T(8,128)(2,1)}, f32[16,8,4096]{2,1,0:T(8,128)}) custom-call(bf16[528,4096]{1,0:T(8,128)(2,1)} %get-tuple-element.9.stream, f32[528,128]{1,0:T(8,128)} %broadcast_in_dim.4.inverse, f32[3,3,4096]{2,1,0:T(4,128)} %feat.5, f32[16,4096]{1,0:T(8,128)} %exponential_bitcast_fusion.rate), custom_call_target="tpu_custom_call" | custom-call | tf_op jit(solution)/shard_map/local_states/pallas_call | solution.py:185
  67.7 0.0 copy-start
  67.7 2.9 %copy.25 = f32[16,8,4096]{2,0,1:T(8,128)S(1)} copy(f32[16,8,4096]{2,1,0:T(8,128)} %get-tuple-element.12) | data formatting | bytes 4194304 | tf_op jit(solution)/shard_map/local_states/pallas_call | solution.py:185
  70.6 0.0 copy-done
  70.6 0.2 fusion.1
  70.8 0.7 copy.45
  71.5 7.9 %all-to-all-start = ((f32[16,16,256]{2,0,1:T(8,128)}), f32[16,16,256]{2,0,1:T(8,128)S(1)}, u32[]{:S(2)}, u32[]{:S(2)}) async-start(f32[16,16,256]{2,0,1:T(8,128)} %bitcast.377), calls=%async_computation | async-start | bytes 524288 | tf_op jit(solution)/shard_map/all_to_all | solution.py:203
  79.4 10.0 %all-to-all-done = f32[16,16,256]{2,0,1:T(8,128)S(1)} async-done(((f32[16,16,256]{2,0,1:T(8,128)}), f32[16,16,256]{2,0,1:T(8,128)S(1)}, u32[]{:S(2)}, u32[]{:S(2)}) %all-to-all-start) | async-done | bytes 262176 | tf_op jit(solution)/shard_map/all_to_all | solution.py:203
  89.8 12.7 %all_to_all.35 = f32[16,16,256]{2,1,0:T(8,128)S(1)} all-to-all(f32[16,16,256]{2,1,0:T(8,128)S(1)} %bitcast.400), channel_id=1, replica_groups=mesh['ctx'=16,'tp'=2] {'ctx'}, dimensions={0} | all-to-all | bytes 524288 | tf_op jit(solution)/shard_map/all_to_all | solution.py:214
  102.5 0.2 copy.34
  102.6 0.3 stack.27
  102.9 0.2 fusion.14
  103.1 0.1 fusion.15
  103.2 0.3 copy.41
  103.5 0.3 stack.34
  103.8 0.3 copy.37
  104.1 0.3 copy.36
  104.3 0.3 copy.38
  104.6 0.3 copy.40
  104.9 0.3 copy.39
  105.2 4.8 %stack.35.states = f32[16,8,4096]{2,1,0:T(8,128)} concatenate(f32[16,1,4096]{2,1,0:T(1,128)S(1)} %stack.27, f32[16,1,4096]{2,1,0:T(1,128)S(1)} %copy.36, f32[16,1,4096]{2,1,0:T(1,128)S(1)} %copy.37, f32[16,1,4096]{2,1,0:T(1,128)S(1)} %copy.38, f32[16,1,4096]{2,1,0:T(1,128)S(1)} %copy.39, f32[16,1,4096]{2,1,0:T(1,128)S(1)} %copy.40, f32[16,1,4096]{2,1,0:T(1,128)S(1)} %copy.41, ...), dimensions={1} | concatenate | bytes 4194304 | tf_op jit(solution)/shard_map/stack | solution.py:218
  109.9 33.7 %long_convolution.1 = bf16[512,4096]{1,0:T(8,128)(2,1)} custom-call(bf16[528,4096]{1,0:T(8,128)(2,1)} %get-tuple-element.9.stream, f32[528,128]{1,0:T(8,128)} %broadcast_in_dim.4.inverse, f32[3,3,4096]{2,1,0:T(4,128)} %feat.5, f32[16,4096]{1,0:T(8,128)} %exponential_bitcast_fusion.rate, f32[16,4096]{1,0:T(8,128)} %bitcast.401, ...), custom_call_target="tpu_custom_call" | custom-call | tf_op jit(solution)/shard_map/long_convolution/pallas_call | solution.py:220
  (19 shorter events, 0.3 us)
Async XLA Ops:
  0.8 4.1 %collective-permute-start = (s32[16]{0:T(128)S(1)}, s32[16]{0:T(128)S(1)}, u32[]{:S(2)}, u32[]{:S(2)}) collective-permute-start(s32[16]{0:T(128)S(1)} %slice_add_fusion), channel_id=1, source_target_pairs={{0,2},{2,4},{4,6},{6,8},{8,10},{10,12},{12,14},{14,16},{16,18},{18... | collective-permute-start | bytes 200 | tf_op jit(solution)/shard_map/ppermute | solution.py:19
  67.7 2.9 %copy-start = (f32[4096,16]{0,1:T(8,128)S(1)}, f32[4096,16]{0,1:T(8,128)}, u32[]{:S(2)}) copy-start(f32[4096,16]{0,1:T(8,128)} %param.14) | copy-start | bytes 786436
  71.5 17.9 %all-to-all-start = ((f32[16,16,256]{2,0,1:T(8,128)}), f32[16,16,256]{2,0,1:T(8,128)S(1)}, u32[]{:S(2)}, u32[]{:S(2)}) async-start(f32[16,16,256]{2,0,1:T(8,128)} %bitcast.377), calls=%async_computation | async-start | bytes 524288 | tf_op jit(solution)/shard_map/all_to_all | solution.py:203

commit v2 on v1

--- a/solution.py
+++ b/solution.py
@@ -62,11 +62,24 @@
             squares[pl.ds(start, count), :] += wide * wide
 
 
-def second_kernel(stream, inverse, feat, rate, product, states, series):
+def segment_scan(first, local, slope, steps):
+    place = lax.broadcasted_iota(jnp.int32, (SEGMENTS, LANES), 0)
+    total = jnp.where(place == 0, first, pltpu.roll(local, 1, 0))
+    reach = 1
+    while reach < SEGMENTS:
+        factor = jnp.exp(slope * float(-steps * reach))
+        total = total + jnp.where(place >= reach, factor * pltpu.roll(total, reach, 0), 0.0)
+        reach *= 2
+    return total
+
+
+def second_kernel(stream, inverse, feat, slope, product, states, whole, series, ends):
     rows = stream.shape[0]
     width = stream.shape[1]
     steps = (rows - HALO) // SEGMENTS
-    modes = rate.shape[0]
+    modes = slope.shape[0]
+    place = lax.broadcasted_iota(jnp.int32, (SEGMENTS, LANES), 0)
+    ahead = ((place - (SEGMENTS - 1)) * steps).astype(jnp.float32)
     for block in range(width // LANES):
         lanes = slice(block * LANES, (block + 1) * LANES)
         taps = [[feat[j, s : s + 1, lanes] for j in range(feat.shape[0])] for s in (1, 2)]
@@ -77,7 +90,8 @@
             rounded = both[start - base :].astype(jnp.bfloat16)
             product[pl.ds(start - HALO, count), lanes] = rounded
             series[block, pl.ds(start - HALO, count), :] = rounded.astype(jnp.float32)
-        rates = [jnp.broadcast_to(rate[m : m + 1, lanes], (SEGMENTS, LANES)) for m in range(modes)]
+        rate = jnp.exp(-slope[:, lanes])
+        rates = [jnp.broadcast_to(rate[m : m + 1], (SEGMENTS, LANES)) for m in range(modes)]
 
         def step(at, held):
             value = series[block, pl.ds(at, SEGMENTS, stride=steps), :]
@@ -87,17 +101,23 @@
         held = lax.fori_loop(0, steps, step, (zero,) * modes, unroll=4)
         for m in range(modes):
             states[m, :, lanes] = held[m]
-
-
-def third_kernel(stream, inverse, feat, rate, weight, product, states, out, series, result):
+            scaled = held[m] * jnp.exp(slope[m : m + 1, lanes] * ahead)
+            ends[m : m + 1, :] = jnp.sum(scaled, axis=0, keepdims=True)
+        whole[0, :, lanes] = ends[...].astype(whole.dtype)
+
+
+def third_kernel(
+    stream, inverse, feat, slope, weight, product, states, entering, out, series, result
+):
     rows = stream.shape[0]
     width = stream.shape[1]
     steps = (rows - HALO) // SEGMENTS
-    modes = rate.shape[0]
+    modes = slope.shape[0]
     for block in range(width // LANES):
         lanes = slice(block * LANES, (block + 1) * LANES)
         series[block] = product[:, lanes].astype(jnp.float32)
-        rates = [jnp.broadcast_to(rate[m : m + 1, lanes], (SEGMENTS, LANES)) for m in range(modes)]
+        rate = jnp.exp(-slope[:, lanes])
+        rates = [jnp.broadcast_to(rate[m : m + 1], (SEGMENTS, LANES)) for m in range(modes)]
         weights = [
             jnp.broadcast_to(weight[m : m + 1, lanes], (SEGMENTS, LANES)) for m in range(modes)
         ]
@@ -113,7 +133,11 @@
             result[block, where, :] = terms[0]
             return held
 
-        first = tuple(states[m, :, lanes] for m in range(modes))
+        arriving = entering[0, :, lanes].astype(jnp.float32)
+        first = tuple(
+            segment_scan(arriving[m : m + 1], states[m, :, lanes], slope[m : m + 1, lanes], steps)
+            for m in range(modes)
+        )
         lax.fori_loop(0, steps, step, first, unroll=4)
         taps = [feat[j, 0:1, lanes] for j in range(feat.shape[0])]
         for base, start, count in block_rows(rows)[1:]:
@@ -123,6 +147,14 @@
             convolved = result[block, pl.ds(start - HALO, count), :]
             total = wide[start - base :] + queries * convolved
             out[pl.ds(start - HALO, count), lanes] = total.astype(jnp.bfloat16)
+
+
+def regrouped(value, groups):
+    if value.shape[0] == groups:
+        return value
+    modes = value.shape[1]
+    flat = jnp.transpose(value, (1, 0, 2)).reshape(modes, groups, -1)
+    return jnp.transpose(flat, (1, 0, 2))
 
 
 def on_device(
@@ -174,35 +206,37 @@
 
     slope = jnp.transpose(decay)
     weight = jnp.transpose(residue)
-    rate = jnp.exp(-slope)
-    size = min(256, channels)
+    share = channels // count
+    size = share if share % LANES == 0 and share <= 512 else min(256, channels)
+    groups = channels // size
     blocks = size // LANES
     stream_spec = pl.BlockSpec((rows, size), lambda c: (0, c))
     inverse_spec = pl.BlockSpec((rows, LANES), lambda c: (0, 0))
     mode_spec = pl.BlockSpec((modes, size), lambda c: (0, c))
     token_spec = pl.BlockSpec((tokens, size), lambda c: (0, c))
     state_spec = pl.BlockSpec((modes, SEGMENTS, size), lambda c: (0, 0, c))
-    product, states = pl.pallas_call(
+    whole_spec = pl.BlockSpec((1, modes, size), lambda c: (c, 0, 0))
+    product, states, whole = pl.pallas_call(
         second_kernel,
         grid=(channels // size,),
         in_specs=[stream_spec, inverse_spec, feat_spec(size), mode_spec],
-        out_specs=[token_spec, state_spec],
+        out_specs=[token_spec, state_spec, whole_spec],
         out_shape=[
             jax.ShapeDtypeStruct((tokens, channels), jnp.bfloat16),
             jax.ShapeDtypeStruct((modes, SEGMENTS, channels), jnp.float32),
-        ],
-        scratch_shapes=[pltpu.VMEM((blocks, tokens, LANES), jnp.float32)],
+            jax.ShapeDtypeStruct((groups, modes, size), jnp.float32),
+        ],
+        scratch_shapes=[
+            pltpu.VMEM((blocks, tokens, LANES), jnp.float32),
+            pltpu.VMEM((modes, LANES), jnp.float32),
+        ],
         compiler_params=params,
         name="local_states",
-    )(stream, inverse, feat_two, rate)
-
-    per_segment = jnp.exp(-slope * float(tokens // SEGMENTS))
-    whole = states[:, 0]
-    for s in range(1, SEGMENTS):
-        whole = per_segment * whole + states[:, s]
-    spread = lax.all_to_all(whole, "ctx", split_axis=1, concat_axis=0, tiled=True)
-    spread = spread.reshape(count, modes, channels // count)
-    share = channels // count
+    )(stream, inverse, feat_two, slope)
+
+    spread = lax.all_to_all(
+        regrouped(whole, count), "ctx", split_axis=0, concat_axis=0, tiled=True
+    ).astype(jnp.float32)
     mine = lax.dynamic_slice_in_dim(slope, lax.axis_index("ctx") * share, share, 1)
     per_shard = jnp.exp(-mine * float(tokens))
     carry = jnp.zeros((modes, share), jnp.float32)
@@ -210,12 +244,10 @@
     for s in range(count):
         carries.append(carry)
         carry = per_shard * carry + spread[s]
-    carried = jnp.concatenate(carries, axis=0)
-    start = lax.all_to_all(carried, "ctx", split_axis=0, concat_axis=1, tiled=True)
-    starts = [start]
-    for s in range(SEGMENTS - 1):
-        starts.append(per_segment * starts[-1] + states[:, s])
-    entering = jnp.stack(starts, axis=1)
+    entering = lax.all_to_all(
+        jnp.stack(carries), "ctx", split_axis=0, concat_axis=0, tiled=True
+    )
+    entering = regrouped(entering, groups)
 
     return pl.pallas_call(
         third_kernel,
@@ -228,6 +260,7 @@
             mode_spec,
             token_spec,
             state_spec,
+            whole_spec,
         ],
         out_specs=token_spec,
         out_shape=jax.ShapeDtypeStruct((tokens, channels), jnp.bfloat16),
@@ -237,7 +270,7 @@
         ],
         compiler_params=params,
         name="long_convolution",
-    )(stream, inverse, feat_two, rate, weight, product, entering)
+    )(stream, inverse, feat_two, slope, weight, product, states, entering)
 
 
 def solution(mesh):

time: 144 us -> 136 us (0.944)
  local copies, waits for them, and re-layouts: 11.5 us -> 0.88 us
  Pallas kernels: 87.6 us -> 89.8 us
  other arithmetic: 6.05 us -> 3.96 us
    another operation x9 -> x0, local copies, waits for them, and re-layouts: 6.9 us -> none  [on_device(): entering = jnp.stack(starts, axis=1)]
    pallas_call x1 -> x0, local copies, waits for them, and re-layouts: 2.85 us -> none  [on_device(): pl.pallas_call(second_kernel, grid=(channels // size,), in_specs=[stream_...]
    exp x1 -> x0, other arithmetic: 1.69 us -> none  [on_device(): rate = jnp.exp(-slope)]
  transfers between devices with their start and end apart: 2 -> 2, of which waited for: 1 -> 2; matrix products, arithmetic and copies ran while one was open for 1% -> 0% of each run, Pallas kernels for 0% -> 0%
where the time goes in v2:
time: 136 us; the launch traced here: 135 us
  Pallas kernels  89.8 us (66%)
  blocking collectives  18.5 us (14%)
  starting transfers between devices  11.1 us (8%)
  waiting for transfers between devices  10.8 us (8%)
  other arithmetic  3.96 us (3%)
    pallas_call x1, Pallas kernels, on_device(): pl.pallas_call(third_kernel, grid=(channels // size,), in_specs=[stream_s...  34.4 us
    pallas_call x1, Pallas kernels, on_device(): pl.pallas_call(first_kernel, grid=(channels // wide,), in_specs=[pl.Block...  31.1 us
    pallas_call x1, Pallas kernels, on_device(): pl.pallas_call(second_kernel, grid=(channels // size,), in_specs=[stream_...  24.3 us
    all_to_all x1, blocking collectives, on_device(): lax.all_to_all(jnp.stack(carries), 'ctx', split_axis=0, concat_axis=0, ti...  13.3 us
    all_to_all x1, waiting for transfers between devices, on_device(): lax.all_to_all(regrouped(whole, count), 'ctx', split_axis=0, concat_axis=...  10 us
    all_to_all x1, starting transfers between devices, on_device(): lax.all_to_all(regrouped(whole, count), 'ctx', split_axis=0, concat_axis=...  8.76 us
    psum x1, blocking collectives, on_device(): summed = lax.psum(jnp.sum(squares, axis=1), 'tp')  5.24 us
  transfers between devices with their start and end apart: 2, of which 2 were waited for; matrix products, arithmetic and copies ran while one was open for 0% of the time, Pallas kernels for 0%

profile of v2, /device:TPU:0, one launch (start us, length us, event | category | flops | bytes accessed | tf_op | source)
XLA Modules:
  0.0 135.3 jit_solution(16810196559784498245)
XLA Ops:
  0.0 0.8 slice_add_fusion
  0.8 2.4 %collective-permute-start = (s32[16]{0:T(128)S(1)}, s32[16]{0:T(128)S(1)}, u32[]{:S(2)}, u32[]{:S(2)}) collective-permute-start(s32[16]{0:T(128)S(1)} %slice_add_fusion), channel_id=1, source_target_pairs={{0,2},{2,4},{4,6},{6,8},{8,10},{10,12},{12,14},{14,16},{16,18},{18... | collective-permute-start | bytes 200 | tf_op jit(solution)/shard_map/ppermute | solution.py:19
  3.1 0.8 collective-permute-done
  4.0 0.8 pad_add_fusion
  4.7 1.0 fusion.one_hot
  5.7 31.1 %first_block.1 = (bf16[528,4096]{1,0:T(8,128)(2,1)}, f32[528,128]{1,0:T(8,128)}) custom-call(bf16[528,512]{1,0:T(8,128)(2,1)} %fusion.one_hot, bf16[512,4096]{1,0:T(8,128)(2,1)} %embed.1, bf16[3,512,4096]{2,1,0:T(8,128)(2,1)} %bitcast.248, f32[3,3,4096]{2,1,0:T(4,128)} %feat.3, f32[7,4096]{1,0:T(8,128)} %inner.1), custom_call_target="tpu_custom_call" | custom-call | tf_op jit(solution)/shard_map/first_block/pallas_call | solution.py:180
  36.8 0.0 copy-start
  36.8 1.2 reduce_sum.9
  38.0 5.2 %psum.7 = f32[528]{0:T(1024)S(1)} all-reduce(f32[528]{0:T(1024)S(1)} %reduce_sum.9), channel_id=1, replica_groups=mesh['ctx'=16,'tp'=2] {'tp'}, use_global_device_ids=true, to_apply=%region_1.0 | all-reduce | flops 528 | bytes 4224 | tf_op jit(solution)/shard_map/psum | solution.py:203
  43.2 0.9 broadcast_in_dim.4.inverse
  44.1 24.3 %local_states.1 = (bf16[512,4096]{1,0:T(8,128)(2,1)}, f32[16,8,4096]{2,1,0:T(8,128)}, f32[16,16,256]{2,1,0:T(8,128)}) custom-call(bf16[528,4096]{1,0:T(8,128)(2,1)} %get-tuple-element.10.stream, f32[528,128]{1,0:T(8,128)} %broadcast_in_dim.4.inverse, f32[3,3,4096]{2,1,0:T(4,128)} %feat.5, f32[16,4096]{1,0:T(8,128)} %bitcast.249), custom_call_target="tpu_custom_call" | custom-call | tf_op jit(solution)/shard_map/local_states/pallas_call | solution.py:219
  68.4 8.8 %all-to-all-start = ((f32[16,16,256]{2,1,0:T(8,128)}), f32[16,16,256]{2,1,0:T(8,128)S(1)}, u32[]{:S(2)}, u32[]{:S(2)}) async-start(f32[16,16,256]{2,1,0:T(8,128)} %get-tuple-element.14), calls=%async_computation | async-start | bytes 524288 | tf_op jit(solution)/shard_map/all_to_all | solution.py:237
  77.1 10.0 %all-to-all-done = f32[16,16,256]{2,1,0:T(8,128)S(1)} async-done(((f32[16,16,256]{2,1,0:T(8,128)}), f32[16,16,256]{2,1,0:T(8,128)S(1)}, u32[]{:S(2)}, u32[]{:S(2)}) %all-to-all-start) | async-done | bytes 262176 | tf_op jit(solution)/shard_map/all_to_all | solution.py:237
  87.1 0.0 copy-done
  87.6 13.3 %all_to_all.10.entering = f32[16,16,256]{2,1,0:T(8,128)} all-to-all(f32[16,16,256]{2,1,0:T(8,128)S(1)} %constant_dynamic-update-slice_fusion), channel_id=1, replica_groups=mesh['ctx'=16,'tp'=2] {'ctx'}, dimensions={0} | all-to-all | bytes 524288 | tf_op jit(solution)/shard_map/all_to_all | solution.py:247
  100.9 34.4 %long_convolution.1 = bf16[512,4096]{1,0:T(8,128)(2,1)} custom-call(bf16[528,4096]{1,0:T(8,128)(2,1)} %get-tuple-element.10.stream, f32[528,128]{1,0:T(8,128)} %broadcast_in_dim.4.inverse, f32[3,3,4096]{2,1,0:T(4,128)} %feat.5, f32[16,4096]{1,0:T(8,128)} %bitcast.250, f32[16,4096]{1,0:T(8,128)} %bitcast.251, bf16[512,4096]{1,0:T(8,128)(2,1)} %get-tuple-element.12.product, ...), custom_call_target="tpu_custom_call" | custom-call | tf_op jit(solution)/shard_map/long_convolution/pallas_call | solution.py:252
  (18 shorter events, 0.3 us)
Async XLA Ops:
  0.8 3.2 %collective-permute-start = (s32[16]{0:T(128)S(1)}, s32[16]{0:T(128)S(1)}, u32[]{:S(2)}, u32[]{:S(2)}) collective-permute-start(s32[16]{0:T(128)S(1)} %slice_add_fusion), channel_id=1, source_target_pairs={{0,2},{2,4},{4,6},{6,8},{8,10},{10,12},{12,14},{14,16},{16,18},{18... | collective-permute-start | bytes 200 | tf_op jit(solution)/shard_map/ppermute | solution.py:19
  36.8 50.4 %copy-start = (f32[4096,16]{0,1:T(8,128)S(1)}, f32[4096,16]{0,1:T(8,128)}, u32[]{:S(2)}) copy-start(f32[4096,16]{0,1:T(8,128)} %param.14) | copy-start | bytes 786436
  68.4 18.8 %all-to-all-start = ((f32[16,16,256]{2,1,0:T(8,128)}), f32[16,16,256]{2,1,0:T(8,128)S(1)}, u32[]{:S(2)}, u32[]{:S(2)}) async-start(f32[16,16,256]{2,1,0:T(8,128)} %get-tuple-element.14), calls=%async_computation | async-start | bytes 524288 | tf_op jit(solution)/shard_map/all_to_all | solution.py:237
